TPU v7x, 256 devices: a whole 4x4x8 slice. The times are simulated.
256 devices in a mesh: seq: 64 (over x, z, core), tp: 4 (over y).
Axes of the slice: x: 4, y: 4, z: 8, core: 2. Of those that a mesh axis runs over, the one named last changes fastest.
Arguments:
- queries: bfloat16 [16384, 4096], P('seq', 'tp'), may hold values from -6 to 6
- keys: bfloat16 [16384, 4096], P('seq', 'tp'), may hold values from -6 to 6
- values: bfloat16 [16384, 4096], P('seq', 'tp'), may hold values from -12 to 12
- seeds: bfloat16 [32, 256], P('tp'), may hold values from -6 to 6
- gain: float32 [4096], P('tp'), may hold values from 0.1 to 1.9
Outputs:
- attended: bfloat16 [16384, 4096], P('seq', 'tp')
All inputs are finite; a program needn't handle non-finite values.
Results may differ from a plain program's by a relative error of at most 0.009.
Values sent between devices are 32-bit elements; how exact they have to be, the bound alone decides.
A program may use at most 192 MiB of HBM per device.

v0:
```python
import jax
import jax.numpy as jnp
from jax import lax
from jax.sharding import PartitionSpec as P


def prefix(value, axis, join, neutral):
    count, mine = (lax.axis_size(axis), lax.axis_index(axis))
    pieces = jax.tree.map(lambda part: lax.all_gather(part, axis), value)
    subtotal = jax.tree.map(
        lambda part, zero: jnp.full_like(part, 0) + jnp.asarray(zero, part.dtype), value, neutral
    )

    def step(position, subtotal):
        longer = join(subtotal, jax.tree.map(lambda part: part[position], pieces))
        return jax.tree.map(lambda new, old: jnp.where(position < mine, new, old), longer, subtotal)

    return lax.fori_loop(0, count - 1, step, subtotal)


def circulant_table(seeds, width):
    heads_here = seeds.shape[0]
    total = seeds.shape[1]
    groups = total // width
    blocks = seeds.reshape(heads_here, groups, width)
    repeated = jnp.tile(blocks, (1, 1, 2 * width - 1))
    square = repeated.reshape(heads_here, groups, width, 2 * width - 1)[:, :, :, :width]
    return jnp.transpose(square, (0, 2, 1, 3)).reshape(heads_here, width, total)


def feature_map(rows, table, heads_here, width):
    count = rows.shape[0]
    x = rows.reshape(count, heads_here, width)
    mixed = jnp.einsum("thj,hjm->thm", x, table, preferred_element_type=jnp.float32) * width ** (
        -0.25
    )
    return (jax.nn.elu(mixed) + 1.0).astype(jnp.bfloat16)


def add_pair(earlier, later):
    return (earlier[0] + later[0], earlier[1] + later[1])


def per_device(queries, keys, values, seeds, gain):
    high = lax.Precision.HIGHEST
    tok = queries.shape[0]
    heads_here = seeds.shape[0]
    feats = seeds.shape[1]
    width = queries.shape[1] // heads_here
    block = min(512, tok)
    count = tok // block
    table = circulant_table(seeds, width)
    causal = jnp.tril(jnp.ones((block, block), dtype=bool))

    def advance(carry, inputs):
        state, totals = carry
        q_rows, k_rows, v_rows = inputs
        fq = feature_map(q_rows, table, heads_here, width)
        fk = feature_map(k_rows, table, heads_here, width)
        vals = v_rows.reshape(block, heads_here, width)
        scores = jnp.einsum("bhm,chm->hbc", fq, fk, preferred_element_type=jnp.float32)
        scores = jnp.where(causal[None], scores, 0.0)
        wscores = scores.astype(jnp.bfloat16)
        num = jnp.einsum("hbc,che->bhe", wscores, vals, preferred_element_type=jnp.float32)
        fq_wide = fq.astype(jnp.float32)
        num = num + jnp.einsum("bhm,hme->bhe", fq_wide, state, precision=high)
        den = jnp.sum(scores, axis=2).T + jnp.einsum("bhm,hm->bh", fq_wide, totals, precision=high)
        state = state + jnp.einsum("chm,che->hme", fk, vals, preferred_element_type=jnp.float32)
        totals = totals + jnp.sum(fk.astype(jnp.float32), axis=0)
        return ((state, totals), (num, den, fq))

    start = (
        jnp.zeros((heads_here, feats, width), jnp.float32),
        jnp.zeros((heads_here, feats), jnp.float32),
    )
    (local_state, local_totals), (num, den, fq) = lax.scan(
        advance,
        start,
        (
            queries.reshape(count, block, -1),
            keys.reshape(count, block, -1),
            values.reshape(count, block, -1),
        ),
    )
    num = num.reshape(tok, heads_here, width)
    den = den.reshape(tok, heads_here)
    fq = fq.reshape(tok, heads_here, feats)
    prior_state, prior_totals = prefix(
        (local_state, local_totals),
        "seq",
        add_pair,
        (jnp.zeros_like(local_state), jnp.zeros_like(local_totals)),
    )
    fq_wide = fq.astype(jnp.float32)
    num = num + jnp.einsum("thm,hme->the", fq_wide, prior_state, precision=high)
    den = den + jnp.einsum("thm,hm->th", fq_wide, prior_totals, precision=high)
    heads = num / den[:, :, None]
    squares = jnp.sum(heads * heads, axis=(1, 2))
    overall = lax.psum(squares, "tp")
    entries = heads_here * width * lax.axis_size("tp")
    factor = lax.rsqrt(overall / entries + 1e-06)
    normed = heads.reshape(tok, heads_here * width) * factor[:, None] * gain[None, :]
    return normed.astype(jnp.bfloat16)


def solution(mesh):
    placed = (P("seq", "tp"), P("seq", "tp"), P("seq", "tp"), P("tp", None), P("tp"))
    return jax.shard_map(
        per_device, mesh=mesh, in_specs=placed, out_specs=P("seq", "tp"), check_vma=False
    )
```

profile of v0, /device:TPU:1, one launch (start us, length us, event | category | flops | bytes accessed | tf_op | source)
XLA Modules:
  0.0 422.0 jit_solution(9573483696206002910)
XLA Ops:
  7.4 3.2 tile.11
  13.7 58.6 %all-gather.1 = f32[512,256]{1,0:T(8,128)} all-gather(f32[8,256]{1,0:T(8,128)S(1)} %get-tuple-element.183), channel_id=3, replica_groups=mesh['seq'=64,'tp'=4] {'seq'}, dimensions={0}, use_global_device_ids=true | all-gather | bytes 532480 | tf_op jit(solution)/shard_map/all_gather | solution.py:9
  72.3 2.5 fusion.2
  76.5 2.2 fusion.8
  78.7 176.8 %all-gather.4.cloned.1.call-done = f32[512,256,128]{2,1,0:T(8,128)} async-done(((f32[8,256,128]{2,1,0:T(8,128)}), f32[512,256,128]{2,1,0:T(8,128)}) %all-gather.4.cloned.1.call-update) | async-done | bytes 67108880 | tf_op jit(solution)/shard_map/all_gather | solution.py:9
  255.6 144.3 %while.10 = (s32[]{:T(128)}, f32[8,256,128]{2,1,0:T(8,128)S(1)}, f32[8,256]{1,0:T(8,128)S(1)}, s32[]{:T(128)}, f32[64,8,256,128]{3,2,1,0:T(8,128)}, /*index=5*/f32[64,8,256]{2,1,0:T(8,128)}, s32[]{:T(128)}, s32[]{:T(128)}) while((s32[]{:T(128)}, f32[8,256,128]{2,1,0:T(8,128)S(1)}, f32[8,256]{1,0:T(8,128)S(1)}, s32[]{:T(128)}, ...), condition=%wide.region_2.3_spmd.clone, body=%wide.region_1.2_spmd.clone.sunk | while | flops 792580 | bytes 3170419 | solution.py:18
  255.6 1.6 add_select_fusion.4
  257.9 1.6 add_select_fusion.4
  260.1 1.6 add_select_fusion.4
  262.4 1.6 add_select_fusion.4
  264.7 1.6 add_select_fusion.4
  267.0 1.6 add_select_fusion.4
  269.3 1.6 add_select_fusion.4
  271.6 1.6 add_select_fusion.4
  273.9 1.6 add_select_fusion.4
  276.2 1.6 add_select_fusion.4
  278.5 1.6 add_select_fusion.4
  280.8 1.6 add_select_fusion.4
  283.0 1.6 add_select_fusion.4
  285.3 1.6 add_select_fusion.4
  287.6 1.6 add_select_fusion.4
  289.9 1.6 add_select_fusion.4
  292.2 1.6 add_select_fusion.4
  294.5 1.6 add_select_fusion.4
  296.8 1.6 add_select_fusion.4
  299.1 1.6 add_select_fusion.4
  301.4 1.6 add_select_fusion.4
  303.7 1.6 add_select_fusion.4
  305.9 1.6 add_select_fusion.4
  308.2 1.6 add_select_fusion.4
  310.5 1.6 add_select_fusion.4
  312.8 1.6 add_select_fusion.4
  315.1 1.6 add_select_fusion.4
  317.4 1.6 add_select_fusion.4
  319.7 1.6 add_select_fusion.4
  322.0 1.6 add_select_fusion.4
  324.3 1.6 add_select_fusion.4
  326.6 1.6 add_select_fusion.4
  328.8 1.6 add_select_fusion.4
  331.1 1.6 add_select_fusion.4
  333.4 1.6 add_select_fusion.4
  335.7 1.6 add_select_fusion.4
  338.0 1.6 add_select_fusion.4
  340.3 1.6 add_select_fusion.4
  342.6 1.6 add_select_fusion.4
  344.9 1.6 add_select_fusion.4
  347.2 1.6 add_select_fusion.4
  349.5 1.6 add_select_fusion.4
  351.7 1.6 add_select_fusion.4
  354.0 1.6 add_select_fusion.4
  356.3 1.6 add_select_fusion.4
  358.6 1.6 add_select_fusion.4
  360.9 1.6 add_select_fusion.4
  363.2 1.6 add_select_fusion.4
  365.5 1.6 add_select_fusion.4
  367.8 1.6 add_select_fusion.4
  370.1 1.6 add_select_fusion.4
  372.4 1.6 add_select_fusion.4
  374.6 1.6 add_select_fusion.4
  376.9 1.6 add_select_fusion.4
  379.2 1.6 add_select_fusion.4
  381.5 1.6 add_select_fusion.4
  400.8 3.4 multiply_reduce_fusion
  405.7 8.5 %psum.7 = f32[256]{0:T(256)S(1)} all-reduce(f32[256]{0:T(256)S(1)} %get-tuple-element.187), channel_id=1, replica_groups=mesh['seq'=64,'tp'=4] {'tp'}, use_global_device_ids=true, to_apply=%region_5.6 | all-reduce | flops 256 | bytes 2048 | tf_op jit(solution)/shard_map/psum | solution.py:99
  (99 shorter events, 64.7 us)
Async XLA Ops:
  6.5 4.1 copy-start
  6.5 249.0 %all-gather.4.cloned.1.call-start = ((), (), s32[]{:S(2)}) async-start(), calls=%async_computation | async-start | bytes 68157440 | tf_op jit(solution)/shard_map/all_gather | solution.py:9
  10.7 1.3 copy-start.4
  10.7 1.4 copy-start.1
  12.0 1.6 copy-start.2
  72.3 3.4 copy-start.3
  404.1 10.0 %copy-start.5 = (f32[1024]{0:T(1024)S(1)}, f32[1024]{0:T(1024)}, u32[]{:S(2)}) copy-start(f32[1024]{0:T(1024)} %param.11) | copy-start | bytes 12292
Sparse Core Ops, SparseCore 0:
  13.7 241.8 all-gather.3
where the time goes:
time: 427 us; the launch traced here: 422 us
  waiting for transfers between devices  177 us (41%)
  other arithmetic  145 us (34%)
  blocking collectives  67.1 us (16%)
  between operations  13.5 us (3%)
  matrix products  13.4 us (3%)
  local copies, waits for them, and re-layouts  5.81 us (1%)
    all_gather x1, waiting for transfers between devices, prefix(): pieces = jax.tree.map(lambda part: lax.all_gather(part, axis), value)  177 us
    select_n x126, other arithmetic, step(): jnp.where(position < mine, new, old)  144 us
    all_gather x1, blocking collectives, prefix(): pieces = jax.tree.map(lambda part: lax.all_gather(part, axis), value)  58.6 us
  transfers between devices with their start and end apart: 1, of which 1 were waited for; matrix products, arithmetic and copies ran while one was open for 2% of the time, Pallas kernels for 0%

commit v1 on v0

v1 whole, which is shorter than its diff:
```python
import functools

import jax
import jax.numpy as jnp
from jax import lax
from jax.experimental import pallas as pl
from jax.experimental.pallas import tpu as pltpu
from jax.sharding import PartitionSpec as P

XS, ZS, CORES, YS = 4, 8, 2, 4
F32, BF16 = jnp.float32, jnp.bfloat16


def remote(src, dst, send, recv, **where):
    return pltpu.make_async_remote_copy(
        src_ref=src,
        dst_ref=dst,
        send_sem=send,
        recv_sem=recv,
        device_id=where,
        device_id_type=pl.DeviceIdType.MESH,
    )


def features(x, table, scale):
    u = jnp.dot(x, table, preferred_element_type=F32) * scale
    return (jnp.maximum(u, 0.0) + jnp.exp(jnp.minimum(u, 0.0))).astype(BF16)


def kernel(
    q_hbm,
    k_hbm,
    v_hbm,
    seeds_ref,
    gain_ref,
    out_ref,
    q,
    k,
    v,
    seedf,
    table,
    fk,
    fq,
    numden,
    heads,
    own,
    got,
    chip,
    up,
    across,
    down,
    back,
    pass_on,
    full,
    tot,
    tot_got,
    tot_chip,
    tot_up,
    tot_row,
    tot_across,
    tot_half,
    norm,
    norm_got,
    load_sem,
    pair_s,
    pair_r,
    up_s,
    up_r,
    x_s,
    x_r,
    down_s,
    down_r,
    fwd_s,
    fwd_r,
    tp_s,
    tp_r,
    tu_s,
    tu_r,
    tx_s,
    tx_r,
    th_s,
    th_r,
    n_s,
    n_r,
):
    tok, columns = q.shape
    heads_here, _, feats = fk.shape
    width = columns // heads_here
    per = heads_here // 2
    rows = own.shape[3]
    scale = width ** (-0.25)
    s = lax.axis_index("seq")
    y = lax.axis_index("tp")
    c = s % CORES
    z = (s // CORES) % ZS
    x = s // (CORES * ZS)
    o = 1 - c

    def at(x_, z_, c_):
        return (x_ * ZS + z_) * CORES + c_

    partner = at(x, z, o)

    def zpeer(d):
        return (z + d) % ZS

    def xpeer(d):
        return (x + d) % XS

    loads = [
        pltpu.make_async_copy(a, b, load_sem.at[i])
        for i, (a, b) in enumerate(((k_hbm, k), (v_hbm, v), (q_hbm, q)))
    ]
    for copy in loads:
        copy.start()

    barrier = pltpu.get_barrier_semaphore()
    mesh_id = pl.DeviceIdType.MESH
    pl.semaphore_signal(barrier, inc=1, device_id={"seq": partner}, device_id_type=mesh_id)
    for d in range(1, ZS):
        pl.semaphore_signal(
            barrier, inc=1, device_id={"seq": at(x, zpeer(d), c)}, device_id_type=mesh_id
        )
    for d in range(1, XS):
        pl.semaphore_signal(
            barrier, inc=1, device_id={"seq": at(xpeer(d), z, c)}, device_id_type=mesh_id
        )
    for d in range(1, YS):
        pl.semaphore_signal(
            barrier, inc=1, device_id={"tp": (y + d) % YS}, device_id_type=mesh_id
        )

    seedf[...] = seeds_ref[...].astype(F32)

    def make_table(h, _):
        row = seedf[pl.ds(h, 1), :]
        parts = []
        for g in range(feats // width):
            part = jnp.broadcast_to(row[:, g * width : (g + 1) * width], (width, width))
            parts.append(pltpu.roll(part, 0, 1, stride=1, stride_axis=0))
        table[h] = jnp.concatenate(parts, axis=1).astype(BF16)
        return 0

    lax.fori_loop(0, heads_here, make_table, 0)
    loads[0].wait()
    loads[1].wait()

    def state_head(phase, i, _):
        h = phase * per + i
        cols = pl.ds(pl.multiple_of(h * width, width), width)
        f = features(k[:, cols], table[h], scale)
        fk[h] = f
        st = lax.dot_general(
            v[:, cols], f, (((0,), (0,)), ((), ())), preferred_element_type=F32
        )
        for half in range(2):
            for part in range(2):
                start = (half * 2 + part) * rows
                own[phase, half, 2 * i + part] = st[start : start + rows]
        tot[pl.ds(h, 1), :] = jnp.sum(f.astype(F32), axis=0, keepdims=True)
        return 0

    pair = [
        remote(own.at[p, o], got.at[p], pair_s.at[p], pair_r.at[p], seq=partner) for p in range(2)
    ]
    tot_pair = remote(tot, tot_got, tp_s, tp_r, seq=partner)
    ups = [
        [
            remote(
                chip.at[p, zpeer(d)],
                up.at[p, z],
                up_s.at[p, d],
                up_r.at[p, d],
                seq=at(x, zpeer(d), c),
            )
            for d in range(1, ZS)
        ]
        for p in range(2)
    ]
    tot_ups = [
        remote(tot_chip, tot_up.at[z], tu_s.at[d], tu_r.at[d], seq=at(x, zpeer(d), c))
        for d in range(1, ZS)
    ]
    xs = [
        [
            remote(
                across.at[p, XS], across.at[p, x], x_s.at[p, d], x_r.at[p, d], seq=at(xpeer(d), z, c)
            )
            for d in range(1, XS)
        ]
        for p in range(2)
    ]
    tot_xs = [
        remote(tot_row, tot_across.at[x], tx_s.at[d], tx_r.at[d], seq=at(xpeer(d), z, c))
        for d in range(1, XS)
    ]
    downs = [
        [
            remote(
                down.at[p, zpeer(d)],
                back.at[p, z],
                down_s.at[p, d],
                down_r.at[p, d],
                seq=at(x, zpeer(d), c),
            )
            for d in range(1, ZS)
        ]
        for p in range(2)
    ]
    tot_fwd = remote(tot_half.at[0], tot_half.at[2], th_s, th_r, seq=partner)
    norms = [
        remote(norm, norm_got.at[y], n_s.at[d], n_r.at[d], tp=(y + d) % YS) for d in range(1, YS)
    ]

    lax.fori_loop(0, per, functools.partial(state_head, 0), 0)
    pl.semaphore_wait(barrier, 1 + (ZS - 1) + (XS - 1) + (YS - 1))
    pair[0].start()
    lax.fori_loop(0, per, functools.partial(state_head, 1), 0)
    pair[1].start()
    tot_pair.start()

    def send_up(p):
        pair[p].wait_recv()
        chip[p] = own[p, c] + got[p]
        for copy in ups[p]:
            copy.start()
        up[p, z] = chip[p, z]

    send_up(0)
    send_up(1)

    tot_pair.wait_recv()
    lanes = feats // 2

    def my_lanes(a):
        return jnp.where(c == 0, a[:, :lanes], a[:, lanes:])

    tot_chip[...] = my_lanes(tot[...] + tot_got[...])
    for copy in tot_ups:
        copy.start()
    tot_up[z] = tot_chip[...]

    loads[2].wait()
    causal = lax.broadcasted_iota(jnp.int32, (tok, tok), 0) >= lax.broadcasted_iota(
        jnp.int32, (tok, tok), 1
    )
    ones = jnp.ones((tok, width), BF16)

    def local_head(h, _):
        cols = pl.ds(pl.multiple_of(h * width, width), width)
        f = features(q[:, cols], table[h], scale)
        fq[h] = f
        scores = lax.dot_general(
            f, fk[h], (((1,), (1,)), ((), ())), preferred_element_type=F32
        )
        weights = jnp.where(causal, scores, 0.0).astype(BF16)
        numden[h] = jnp.dot(
            weights, jnp.concatenate([v[:, cols], ones], axis=1), preferred_element_type=F32
        )
        return 0

    def send_across(p):
        for copy in ups[p]:
            copy.wait_recv()
        total = up[p, 0]
        for i in range(1, ZS):
            total = total + up[p, i]
        across[p, XS] = total
        for copy in xs[p]:
            copy.start()
        across[p, x] = jnp.zeros_like(total)

    def send_down(p):
        for copy in xs[p]:
            copy.wait_recv()
        run = jnp.zeros((rows, feats), F32)
        for i in range(XS):
            run = run + jnp.where(i < x, across[p, i], 0.0)
        for i in range(ZS):
            down[p, i] = run
            if i < ZS - 1:
                run = run + up[p, i]
        for copy in downs[p]:
            copy.start()
        back[p, z] = down[p, z]

    lax.fori_loop(0, per, local_head, 0)
    send_across(0)
    lax.fori_loop(per, heads_here, local_head, 0)

    for copy in tot_ups:
        copy.wait_recv()
    run = jnp.zeros((heads_here, lanes), F32)
    before = run
    for i in range(ZS):
        before = before + jnp.where(i < z, tot_up[i], 0.0)
        run = run + tot_up[i]
    tot_row[...] = run
    for copy in tot_xs:
        copy.start()
    tot_across[x] = jnp.zeros_like(run)

    send_down(0)
    send_across(1)

    for copy in tot_xs:
        copy.wait_recv()
    for i in range(XS):
        before = before + jnp.where(i < x, tot_across[i], 0.0)
    tot_half[1] = before + jnp.where(c == 1, my_lanes(tot_got[...]), 0.0)
    tot_half[0] = before + jnp.where(c == 0, my_lanes(tot[...]), 0.0)
    tot_fwd.start()

    send_down(1)

    def piece(p, j):
        return remote(
            pass_on.at[p, j], full.at[p, c, j], fwd_s.at[p, j], fwd_r.at[p, j], seq=partner
        )

    def send_on(p):
        def one(j):
            base = back[p, j]
            pass_on[p, j] = base + jnp.where(c == 0, own[p, 0, j], 0.0)
            piece(p, j).start()
            full[p, c, j] = base + jnp.where(c == 1, got[p, j], 0.0)

        one(z)
        for d in range(1, ZS):
            downs[p][d - 1].wait_recv()
            one((z - d + ZS) % ZS)

    def finish(p):
        for j in range(ZS):
            piece(p, j).wait_recv()
        first, second = tot_half[1], tot_half[2]
        totals = jnp.concatenate(
            [jnp.where(c == 0, first, second), jnp.where(c == 0, second, first)], axis=1
        )
        seedf[...] = totals

        def head(i, acc):
            h = p * per + i
            parts = [
                full[p, half, 2 * i + part].astype(BF16) for half in range(2) for part in range(2)
            ]
            row = seedf[pl.ds(h, 1), :]
            parts.append(jnp.broadcast_to(row, (width, feats)).astype(BF16))
            prior = jnp.concatenate(parts, axis=0)
            nd = numden[h] + lax.dot_general(
                fq[h], prior, (((1,), (1,)), ((), ())), preferred_element_type=F32
            )
            out = nd[:, :width] / nd[:, width:]
            heads[h] = out
            return acc + out * out

        return head

    send_on(0)
    acc = jnp.zeros((tok, width), F32)
    tot_fwd.wait_recv()
    acc = lax.fori_loop(0, per, finish(0), acc)
    send_on(1)
    acc = lax.fori_loop(0, per, finish(1), acc)

    sums = jnp.sum(acc.T, axis=0, keepdims=True)
    norm[...] = jnp.broadcast_to(sums, norm.shape)
    for copy in norms:
        copy.start()
    norm_got[y] = norm[...]
    for copy in norms:
        copy.wait_recv()
    overall = norm_got[0]
    for i in range(1, YS):
        overall = overall + norm_got[i]
    factor = lax.rsqrt(overall / (columns * YS) + 1e-06)
    factor = jnp.broadcast_to(factor[:1], (width, tok)).T

    def scale_head(h, _):
        cols = pl.ds(pl.multiple_of(h * width, width), width)
        out_ref[:, cols] = (heads[h] * factor * gain_ref[pl.ds(h, 1), :]).astype(BF16)
        return 0

    lax.fori_loop(0, heads_here, scale_head, 0)

    for p in range(2):
        pair[p].wait_send()
        for copy in ups[p] + xs[p] + downs[p]:
            copy.wait_send()
        for j in range(ZS):
            piece(p, j).wait_send()
    tot_pair.wait_send()
    tot_fwd.wait_send()
    for copy in tot_ups + tot_xs + norms:
        copy.wait_send()


def per_device(queries, keys, values, seeds, gain):
    tok, columns = queries.shape
    heads_here, feats = seeds.shape
    width = columns // heads_here
    per = heads_here // 2
    rows = per * width // (2 * ZS)
    dma = pltpu.SemaphoreType.DMA
    vm = pltpu.VMEM
    hbm = pl.BlockSpec(memory_space=pl.ANY)
    onchip = pl.BlockSpec(memory_space=pltpu.VMEM)
    return pl.pallas_call(
        kernel,
        out_shape=jax.ShapeDtypeStruct((tok, columns), BF16),
        in_specs=[hbm, hbm, hbm, onchip, onchip],
        out_specs=onchip,
        scratch_shapes=[
            vm((tok, columns), BF16),
            vm((tok, columns), BF16),
            vm((tok, columns), BF16),
            vm((heads_here, feats), F32),
            vm((heads_here, width, feats), BF16),
            vm((heads_here, tok, feats), BF16),
            vm((heads_here, tok, feats), BF16),
            vm((heads_here, tok, 2 * width), F32),
            vm((heads_here, tok, width), F32),
            vm((2, 2, ZS, rows, feats), F32),
            vm((2, ZS, rows, feats), F32),
            vm((2, ZS, rows, feats), F32),
            vm((2, ZS, rows, feats), F32),
            vm((2, XS + 1, rows, feats), F32),
            vm((2, ZS, rows, feats), F32),
            vm((2, ZS, rows, feats), F32),
            vm((2, ZS, rows, feats), F32),
            vm((2, 2, ZS, rows, feats), F32),
            vm((heads_here, feats), F32),
            vm((heads_here, feats), F32),
            vm((heads_here, feats // 2), F32),
            vm((ZS, heads_here, feats // 2), F32),
            vm((heads_here, feats // 2), F32),
            vm((XS, heads_here, feats // 2), F32),
            vm((3, heads_here, feats // 2), F32),
            vm((8, tok), F32),
            vm((YS, 8, tok), F32),
            dma((3,)),
            dma((2,)),
            dma((2,)),
            dma((2, ZS)),
            dma((2, ZS)),
            dma((2, XS)),
            dma((2, XS)),
            dma((2, ZS)),
            dma((2, ZS)),
            dma((2, ZS)),
            dma((2, ZS)),
            dma,
            dma,
            dma((ZS,)),
            dma((ZS,)),
            dma((XS,)),
            dma((XS,)),
            dma,
            dma,
            dma((YS,)),
            dma((YS,)),
        ],
        compiler_params=pltpu.CompilerParams(collective_id=0, has_side_effects=True),
        name="prefix_attention",
    )(queries, keys, values, seeds, gain.reshape(heads_here, width))


def solution(mesh):
    placed = (P("seq", "tp"), P("seq", "tp"), P("seq", "tp"), P("tp", None), P("tp"))
    return jax.shard_map(
        per_device, mesh=mesh, in_specs=placed, out_specs=P("seq", "tp"), check_vma=False
    )
```

time: 427 us -> 50 us (0.12); the launches traced: 422 us -> 49.8 us
  waiting for transfers between devices: 177 us -> 0 us
  other arithmetic: 145 us -> 0 us
  blocking collectives: 67.1 us -> 0 us
  Pallas kernels: 0 us -> 47.9 us
  between operations: 13.5 us -> 0.01 us
  matrix products: 13.4 us -> 0 us
    all_gather x1 -> x0, waiting for transfers between devices: 177 us -> none  [prefix(): pieces = jax.tree.map(lambda part: lax.all_gather(part, axis), value)]
    select_n x126 -> x0, other arithmetic: 144 us -> none  [step(): jnp.where(position < mine, new, old)]
    all_gather x1 -> x0, blocking collectives: 58.6 us -> none  [prefix(): pieces = jax.tree.map(lambda part: lax.all_gather(part, axis), value)]
    pallas_call x0 -> x1, Pallas kernels: none -> 47.9 us  [per_device(): pl.pallas_call(kernel, out_shape=jax.ShapeDtypeStruct((tok, columns), BF1...]
    dot_general x9 -> x0, matrix products: 13.4 us -> none  [the longest x2 3.72 us: feature_map(): jnp.einsum('thj,hjm->thm', x, table, preferred_element_type=jnp.float32)]
    psum x1 -> x0, blocking collectives: 8.46 us -> none  [per_device(): overall = lax.psum(squares, 'tp')]
  transfers between devices with their start and end apart: 1 -> 0, of which waited for: 1 -> 0; matrix products, arithmetic and copies ran while one was open for 2% -> 0% of each run, Pallas kernels for 0% -> 0%
where the time goes in v1:
time: 50 us; the launch traced here: 49.8 us
  Pallas kernels  47.9 us (96%)
  local copies, waits for them, and re-layouts  1.87 us (4%)
    pallas_call x1, Pallas kernels, per_device(): pl.pallas_call(kernel, out_shape=jax.ShapeDtypeStruct((tok, columns), BF1...  47.9 us
    unnamed x1, local copies, waits for them, and re-layouts  1.87 us

profile of v1, /device:TPU:1, one launch (start us, length us, event | category | flops | bytes accessed | tf_op | source)
XLA Modules:
  0.0 49.8 jit_solution(6893822581401707080)
XLA Ops:
  0.0 47.9 %prefix_attention.1 = bf16[256,1024]{1,0:T(8,128)(2,1)} custom-call(bf16[256,1024]{1,0:T(8,128)(2,1)} %q_hbm.1, bf16[256,1024]{1,0:T(8,128)(2,1)} %k_hbm.1, bf16[256,1024]{1,0:T(8,128)(2,1)} %v_hbm.1, bf16[8,256]{1,0:T(8,128)(2,1)} %seeds_ref.1, f32[8,128]{1,0:T(8,128)} %bitcast.1), custom_call_target="tpu_custom_call" | custom-call | tf_op jit(solution)/shard_map/prefix_attention/pallas_call | solution.py:408
  47.9 1.9 %copy.7 = bf16[256,1024]{1,0:T(8,128)(2,1)} copy(bf16[256,1024]{1,0:T(8,128)(2,1)} %prefix_attention.1) | data formatting | bytes 1048576

commit v2 on v1

v2 whole, which is shorter than its diff:
```python
import functools

import jax
import jax.numpy as jnp
from jax import lax
from jax.experimental import pallas as pl
from jax.experimental.pallas import tpu as pltpu
from jax.sharding import PartitionSpec as P

XS, ZS, CORES, YS = 4, 8, 2, 4
PHASES = 4
FAR_FIRST = (4, 3, 5, 2, 6, 1, 7)
TOTALS = PHASES // 2 - 1
F32, BF16 = jnp.float32, jnp.bfloat16


def remote(src, dst, send, recv, **where):
    return pltpu.make_async_remote_copy(
        src_ref=src,
        dst_ref=dst,
        send_sem=send,
        recv_sem=recv,
        device_id=where,
        device_id_type=pl.DeviceIdType.MESH,
    )


def features(x, table, scale):
    u = jnp.dot(x, table, preferred_element_type=F32) * scale
    return (jnp.maximum(u, 0.0) + jnp.exp(jnp.minimum(u, 0.0))).astype(BF16)


def kernel(
    q_hbm,
    k_hbm,
    v_hbm,
    seeds_ref,
    heads,
    factor_ref,
    q,
    k,
    v,
    seedf,
    table,
    fk,
    fq,
    numden,
    own,
    got,
    chip,
    up,
    across,
    down,
    back,
    pass_on,
    full,
    tot,
    tot_got,
    tot_chip,
    tot_up,
    tot_across,
    tot_down,
    tot_back,
    tot_on,
    tot_full,
    norm,
    load_sem,
    pair_s,
    pair_r,
    up_s,
    up_r,
    x_s,
    x_r,
    down_s,
    down_r,
    fwd_s,
    fwd_r,
    tp_s,
    tp_r,
    tu_s,
    tu_r,
    tx_s,
    tx_r,
    td_s,
    td_r,
    th_s,
    th_r,
    n_s,
    n_r,
):
    tok, columns = q.shape
    heads_here, _, feats = fk.shape
    width = columns // heads_here
    per = heads_here // PHASES
    rows = own.shape[3]
    blocks = ZS // per
    lanes = feats // 2
    scale = width ** (-0.25)
    s = lax.axis_index("seq")
    y = lax.axis_index("tp")
    c = s % CORES
    z = (s // CORES) % ZS
    x = s // (CORES * ZS)
    o = 1 - c

    def at(x_, z_, c_):
        return (x_ * ZS + z_) * CORES + c_

    partner = at(x, z, o)

    def zpeer(d):
        return (z + d) % ZS

    def xpeer(d):
        return (x + d) % XS

    def chunk(p):
        return slice(p * per * width, (p + 1) * per * width)

    k_loads = [
        pltpu.make_async_copy(k_hbm.at[:, chunk(p)], k.at[:, chunk(p)], load_sem.at[0, p])
        for p in range(PHASES)
    ]
    v_loads = [
        pltpu.make_async_copy(v_hbm.at[:, chunk(p)], v.at[:, chunk(p)], load_sem.at[1, p])
        for p in range(PHASES)
    ]
    q_load = pltpu.make_async_copy(q_hbm, q, load_sem.at[2, 0])
    for p in range(PHASES):
        k_loads[p].start()
        v_loads[p].start()
    q_load.start()

    barrier = pltpu.get_barrier_semaphore()
    mesh_id = pl.DeviceIdType.MESH
    pl.semaphore_signal(barrier, inc=1, device_id={"seq": partner}, device_id_type=mesh_id)
    for d in FAR_FIRST:
        pl.semaphore_signal(
            barrier, inc=1, device_id={"seq": at(x, zpeer(d), c)}, device_id_type=mesh_id
        )
    for d in range(1, XS):
        pl.semaphore_signal(
            barrier, inc=1, device_id={"seq": at(xpeer(d), z, c)}, device_id_type=mesh_id
        )
    for d in range(1, YS):
        pl.semaphore_signal(
            barrier, inc=1, device_id={"tp": (y + d) % YS}, device_id_type=mesh_id
        )

    seedf[...] = seeds_ref[...].astype(F32)

    def make_table(h):
        row = seedf[pl.ds(h, 1), :]
        parts = []
        for g in range(feats // width):
            part = jnp.broadcast_to(row[:, g * width : (g + 1) * width], (width, width))
            parts.append(pltpu.roll(part, 0, 1, stride=1, stride_axis=0))
        return jnp.concatenate(parts, axis=1).astype(BF16)

    def state_head(phase, i, _):
        h = phase * per + i
        cols = pl.ds(pl.multiple_of(h * width, width), width)
        circulant = make_table(h)
        table[h] = circulant
        f = features(k[:, cols], circulant, scale)
        fk[h] = f
        st = lax.dot_general(
            v[:, cols], f, (((0,), (0,)), ((), ())), preferred_element_type=F32
        )
        for half in range(2):
            for b in range(blocks):
                start = (half * blocks + b) * rows
                own[phase, half, blocks * i + b] = st[start : start + rows]
        sums = jnp.sum(f.astype(F32), axis=0, keepdims=True)
        for half in range(2):
            tot[half, h] = sums[:, half * lanes : (half + 1) * lanes]
        return 0

    everyone = range(PHASES)
    pair = [
        remote(own.at[p, o], got.at[p], pair_s.at[p], pair_r.at[p], seq=partner) for p in everyone
    ]
    tot_pair = remote(tot, tot_got, tp_s, tp_r, seq=partner)

    def over_z(src, dst, slot, send, recv):
        copies = [
            remote(src.at[zpeer(d)], dst.at[slot], send, recv, seq=at(x, zpeer(d), c))
            for d in FAR_FIRST
        ]
        all_but_one = pl.ds(0, ZS - 1)
        whole = remote(src.at[all_but_one], dst.at[all_but_one], send, recv, seq=partner)
        return copies, whole

    def over_x(slots, send, recv):
        copies = [
            remote(slots.at[XS], slots.at[x], send, recv, seq=at(xpeer(d), z, c)) for d in (2, 1, 3)
        ]
        all_but_one = pl.ds(0, XS - 1)
        whole = remote(slots.at[all_but_one], slots.at[all_but_one], send, recv, seq=partner)
        return copies, whole

    ups = [over_z(chip.at[p], up.at[p], z, up_s.at[p], up_r.at[p]) for p in everyone]
    xs = [over_x(across.at[p], x_s.at[p], x_r.at[p]) for p in everyone]
    downs = [over_z(down.at[p], back.at[p], z, down_s.at[p], down_r.at[p]) for p in everyone]
    forwards = [
        remote(pass_on.at[p], full.at[p, c], fwd_s.at[p], fwd_r.at[p], seq=partner)
        for p in everyone
    ]
    tot_ups = over_z(tot_chip, tot_up, z, tu_s, tu_r)
    tot_xs = over_x(tot_across, tx_s, tx_r)
    tot_downs = over_z(tot_down, tot_back, z, td_s, td_r)
    tot_fwd = remote(tot_on, tot_full.at[c], th_s, th_r, seq=partner)
    norms = [
        remote(norm.at[YS], norm.at[y], n_s, n_r, tp=(y + d) % YS) for d in (2, 1, 3)
    ]
    norm_whole = remote(
        norm.at[pl.ds(0, YS - 1)], norm.at[pl.ds(0, YS - 1)], n_s, n_r, seq=partner
    )

    def start(copies):
        for copy in copies[0]:
            copy.start()

    def arrive(copies):
        copies[1].wait_recv()

    def sent(copies):
        copies[1].wait_send()

    def states(p):
        k_loads[p].wait()
        v_loads[p].wait()
        lax.fori_loop(0, per, functools.partial(state_head, p), 0)
        if p == 0:
            pl.semaphore_wait(barrier, 1 + (ZS - 1) + (XS - 1) + (YS - 1))
        pair[p].start()

    def send_up(p):
        pair[p].wait_recv()
        chip[p] = own[p, c] + got[p]
        start(ups[p])
        up[p, z] = chip[p, z]

    def gather_row(copies, arrived, total, own_slot, cross):
        arrive(copies)
        t = arrived[0]
        for i in range(1, ZS):
            t = t + arrived[i]
        total[...] = t
        start(cross)
        own_slot[...] = jnp.zeros_like(t)

    def give_back(cross, slots, arrived, result, own_slot, copies):
        arrive(cross)
        base = jnp.where(0 < x, slots[0], 0.0)
        for i in range(1, XS):
            base = base + jnp.where(i < x, slots[i], 0.0)
        for i in range(ZS):
            result[i] = base
            if i < ZS - 1:
                base = base + arrived[i]
        start(copies)
        own_slot[...] = result[z]

    def send_across(p):
        gather_row(ups[p], up.at[p], across.at[p, XS], across.at[p, x], xs[p])

    def send_down(p):
        give_back(xs[p], across.at[p], up.at[p], down.at[p], back.at[p, z], downs[p])

    ones = jnp.ones((tok, width), BF16)

    def local_head(h, _):
        cols = pl.ds(pl.multiple_of(h * width, width), width)
        f = features(q[:, cols], table[h], scale)
        fq[h] = f
        scores = lax.dot_general(
            f, fk[h], (((1,), (1,)), ((), ())), preferred_element_type=F32
        )
        causal = lax.broadcasted_iota(jnp.int32, (tok, tok), 0) >= lax.broadcasted_iota(
            jnp.int32, (tok, tok), 1
        )
        weights = jnp.where(causal, scores, 0.0).astype(BF16)
        numden[h] = jnp.dot(
            weights, jnp.concatenate([v[:, cols], ones], axis=1), preferred_element_type=F32
        )
        return 0

    def local_heads(first, last):
        lax.fori_loop(first, last, local_head, 0)

    def send_on(p):
        arrive(downs[p])
        base = back[p]
        pass_on[p] = base + jnp.where(c == 0, own[p, 0], 0.0)
        forwards[p].start()
        full[p, c] = base + jnp.where(c == 1, got[p], 0.0)

    def finish(p, acc):
        forwards[p].wait_recv()

        def head(i, acc):
            h = p * per + i
            parts = [
                full[p, half, blocks * i + b].astype(BF16)
                for half in range(2)
                for b in range(blocks)
            ]
            row = jnp.concatenate([tot_full[0, h], tot_full[1, h]], axis=1)
            parts.append(jnp.broadcast_to(row, (width, feats)).astype(BF16))
            prior = jnp.concatenate(parts, axis=0)
            nd = numden[h] + lax.dot_general(
                fq[h], prior, (((1,), (1,)), ((), ())), preferred_element_type=F32
            )
            out = nd[:, :width] / nd[:, width:]
            heads[h] = out
            return acc + out * out

        return lax.fori_loop(0, per, head, acc)

    states(0)
    states(1)
    for p in range(2, PHASES):
        send_up(p - 2)
        states(p)
    tot_pair.start()
    send_up(PHASES - 2)
    tot_pair.wait_recv()
    tot_chip[...] = tot[c] + tot_got[c]
    start(tot_ups)
    tot_up[z] = tot_chip[z]
    send_up(PHASES - 1)

    q_load.wait()
    local_heads(0, heads_here - 2)
    for copy in pair + [tot_pair]:
        copy.wait_send()
    send_across(0)
    local_heads(heads_here - 2, heads_here)
    for p in range(1, PHASES):
        if p == PHASES - 1:
            gather_row(tot_ups, tot_up, tot_across.at[XS], tot_across.at[x], tot_xs)
        send_across(p)
        sent(ups[p - 1])
        if p == PHASES - 1:
            give_back(tot_xs, tot_across, tot_up, tot_down, tot_back.at[z], tot_downs)
        send_down(p - 1)
        sent(xs[p - 1])
    for copies in (ups[PHASES - 1], tot_ups, tot_xs):
        sent(copies)
    send_down(PHASES - 1)
    sent(xs[PHASES - 1])

    acc = jnp.zeros((tok, width), F32)
    for p in range(PHASES):
        send_on(p)
        if p == TOTALS:
            arrive(tot_downs)
            tot_on[...] = tot_back[...] + jnp.where(c == 0, tot[0], 0.0)
            tot_fwd.start()
            tot_full[c] = tot_back[...] + jnp.where(c == 1, tot_got[1], 0.0)
            sent(tot_downs)
        if p == TOTALS + 1:
            tot_fwd.wait_recv()
            for r in range(p):
                acc = finish(r, acc)
        if p > TOTALS + 1:
            acc = finish(p - 1, acc)
        sent(downs[p])
    for p in range(PHASES - 1):
        forwards[p].wait_send()
    tot_fwd.wait_send()
    acc = finish(PHASES - 1, acc)

    sums = jnp.sum(acc.T, axis=0, keepdims=True)
    norm[YS] = jnp.broadcast_to(sums, norm.shape[1:])
    for copy in norms:
        copy.start()
    norm[y] = norm[YS]
    norm_whole.wait_recv()
    overall = norm[0]
    for i in range(1, YS):
        overall = overall + norm[i]
    factor = lax.rsqrt(overall / (columns * YS) + 1e-06)
    factor = jnp.broadcast_to(factor[:1], (width, tok)).T

    factor_ref[...] = factor

    forwards[PHASES - 1].wait_send()
    norm_whole.wait_send()


def normalize(heads, factor, gain, out_hbm, out, sems):
    heads_here, _, width = heads.shape
    copies = []
    scale = factor[...]
    for h in range(heads_here):
        cols = slice(h * width, (h + 1) * width)
        out[:, cols] = (heads[h] * scale * gain[h : h + 1, :]).astype(BF16)
        copies.append(pltpu.make_async_copy(out.at[:, cols], out_hbm.at[:, cols], sems.at[h]))
        copies[-1].start()
    for copy in copies:
        copy.wait()


def per_device(queries, keys, values, seeds, gain):
    tok, columns = queries.shape
    heads_here, feats = seeds.shape
    width = columns // heads_here
    per = heads_here // PHASES
    rows = per * width // (2 * ZS)
    dma = pltpu.SemaphoreType.DMA
    vm = pltpu.VMEM
    hbm = pl.BlockSpec(memory_space=pl.ANY)
    onchip = pl.BlockSpec(memory_space=pltpu.VMEM)
    half = (heads_here, 1, feats // 2)
    heads, factor = pl.pallas_call(
        kernel,
        out_shape=(vm((heads_here, tok, width), F32), vm((tok, width), F32)),
        in_specs=[hbm, hbm, hbm, onchip],
        out_specs=(onchip, onchip),
        scratch_shapes=[
            vm((tok, columns), BF16),
            vm((tok, columns), BF16),
            vm((tok, columns), BF16),
            vm((heads_here, feats), F32),
            vm((heads_here, width, feats), BF16),
            vm((heads_here, tok, feats), BF16),
            vm((heads_here, tok, feats), BF16),
            vm((heads_here, tok, 2 * width), F32),
            vm((PHASES, 2, ZS, rows, feats), F32),
            vm((PHASES, ZS, rows, feats), F32),
            vm((PHASES, ZS, rows, feats), F32),
            vm((PHASES, ZS, rows, feats), F32),
            vm((PHASES, XS + 1, rows, feats), F32),
            vm((PHASES, ZS, rows, feats), F32),
            vm((PHASES, ZS, rows, feats), F32),
            vm((PHASES, ZS, rows, feats), F32),
            vm((PHASES, 2, ZS, rows, feats), F32),
            vm((2,) + half, F32),
            vm((2,) + half, F32),
            vm(half, F32),
            vm((ZS,) + half[1:], F32),
            vm((XS + 1,) + half[1:], F32),
            vm((ZS,) + half[1:], F32),
            vm((ZS,) + half[1:], F32),
            vm(half, F32),
            vm((2,) + half, F32),
            vm((YS + 1, 8, tok), F32),
            dma((3, PHASES)),
            dma((PHASES,)),
            dma((PHASES,)),
            dma((PHASES,)),
            dma((PHASES,)),
            dma((PHASES,)),
            dma((PHASES,)),
            dma((PHASES,)),
            dma((PHASES,)),
            dma((PHASES,)),
            dma((PHASES,)),
            dma,
            dma,
            dma,
            dma,
            dma,
            dma,
            dma,
            dma,
            dma,
            dma,
            dma,
            dma,
        ],
        compiler_params=pltpu.CompilerParams(collective_id=0, has_side_effects=True),
        name="prefix_attention",
    )(queries, keys, values, seeds)
    return pl.pallas_call(
        normalize,
        out_shape=jax.ShapeDtypeStruct((tok, columns), BF16),
        in_specs=[onchip, onchip, onchip],
        out_specs=hbm,
        scratch_shapes=[vm((tok, columns), BF16), dma((heads_here,))],
        name="normalize",
    )(
        pltpu.with_memory_space_constraint(heads, pltpu.VMEM),
        pltpu.with_memory_space_constraint(factor, pltpu.VMEM),
        gain.reshape(heads_here, width),
    )


def solution(mesh):
    placed = (P("seq", "tp"), P("seq", "tp"), P("seq", "tp"), P("tp", None), P("tp"))
    return jax.shard_map(
        per_device, mesh=mesh, in_specs=placed, out_specs=P("seq", "tp"), check_vma=False
    )
```

time: 50 us -> 44 us (0.88)
  Pallas kernels: 47.9 us -> 43.8 us
  local copies, waits for them, and re-layouts: 1.87 us -> 0 us
    pallas_call x1 -> x2, Pallas kernels: 47.9 us -> 43.8 us  [the longest x1 42.3 us: per_device(): pl.pallas_call(kernel, out_shape=(vm((heads_here, tok, width), F32), vm((...]
    unnamed x1 -> x0, local copies, waits for them, and re-layouts: 1.87 us -> none
where the time goes in v2:
time: 44 us; the launch traced here: 43.8 us
  Pallas kernels  43.8 us (100%)
    pallas_call x1, Pallas kernels, per_device(): pl.pallas_call(kernel, out_shape=(vm((heads_here, tok, width), F32), vm((...  42.3 us
    pallas_call x1, Pallas kernels, per_device(): pl.pallas_call(normalize, out_shape=jax.ShapeDtypeStruct((tok, columns),...  1.57 us

profile of v2, /device:TPU:1, one launch (start us, length us, event | category | flops | bytes accessed | tf_op | source)
XLA Modules:
  0.0 43.8 jit_solution(13682606879107985853)
XLA Ops:
  0.0 42.3 %prefix_attention.1 = (f32[8,256,128]{2,1,0:T(8,128)S(1)}, f32[256,128]{1,0:T(8,128)S(1)}) custom-call(bf16[256,1024]{1,0:T(8,128)(2,1)} %q_hbm.1, bf16[256,1024]{1,0:T(8,128)(2,1)} %k_hbm.1, bf16[256,1024]{1,0:T(8,128)(2,1)} %v_hbm.1, bf16[8,256]{1,0:T(8,128)(2,1)} %seeds_ref.1), custom_call_target="tpu_custom_call" | custom-call | tf_op jit(solution)/shard_map/prefix_attention/pallas_call | solution.py:417
  42.3 1.6 %normalize.1 = bf16[256,1024]{1,0:T(8,128)(2,1)} custom-call(f32[8,256,128]{2,1,0:T(8,128)S(1)} %get-tuple-element.7.heads, f32[256,128]{1,0:T(8,128)S(1)} %get-tuple-element.8.factor, f32[8,128]{1,0:T(8,128)} %bitcast.1), custom_call_target="tpu_custom_call" | custom-call | tf_op jit(solution)/shard_map/normalize/pallas_call | solution.py:477

commit v3 on v2

--- a/solution.py
+++ b/solution.py
@@ -35,6 +35,7 @@
     k_hbm,
     v_hbm,
     seeds_ref,
+    gain_ref,
     heads,
     factor_ref,
     q,
@@ -98,9 +99,9 @@
     scale = width ** (-0.25)
     s = lax.axis_index("seq")
     y = lax.axis_index("tp")
-    c = s % CORES
-    z = (s // CORES) % ZS
-    x = s // (CORES * ZS)
+    c = lax.rem(s, CORES)
+    z = lax.rem(lax.div(s, CORES), ZS)
+    x = lax.div(s, CORES * ZS)
     o = 1 - c
 
     def at(x_, z_, c_):
@@ -109,10 +110,10 @@
     partner = at(x, z, o)
 
     def zpeer(d):
-        return (z + d) % ZS
+        return lax.rem(z + d, ZS)
 
     def xpeer(d):
-        return (x + d) % XS
+        return lax.rem(x + d, XS)
 
     def chunk(p):
         return slice(p * per * width, (p + 1) * per * width)
@@ -144,7 +145,7 @@
         )
     for d in range(1, YS):
         pl.semaphore_signal(
-            barrier, inc=1, device_id={"tp": (y + d) % YS}, device_id_type=mesh_id
+            barrier, inc=1, device_id={"tp": lax.rem(y + d, YS)}, device_id_type=mesh_id
         )
 
     seedf[...] = seeds_ref[...].astype(F32)
@@ -211,7 +212,7 @@
     tot_downs = over_z(tot_down, tot_back, z, td_s, td_r)
     tot_fwd = remote(tot_on, tot_full.at[c], th_s, th_r, seq=partner)
     norms = [
-        remote(norm.at[YS], norm.at[y], n_s, n_r, tp=(y + d) % YS) for d in (2, 1, 3)
+        remote(norm.at[YS], norm.at[y], n_s, n_r, tp=lax.rem(y + d, YS)) for d in (2, 1, 3)
     ]
     norm_whole = remote(
         norm.at[pl.ds(0, YS - 1)], norm.at[pl.ds(0, YS - 1)], n_s, n_r, seq=partner
@@ -230,7 +231,7 @@
     def states(p):
         k_loads[p].wait()
         v_loads[p].wait()
-        lax.fori_loop(0, per, functools.partial(state_head, p), 0)
+        lax.fori_loop(0, per, functools.partial(state_head, p), 0, unroll=True)
         if p == 0:
             pl.semaphore_wait(barrier, 1 + (ZS - 1) + (XS - 1) + (YS - 1))
         pair[p].start()
@@ -313,7 +314,7 @@
                 fq[h], prior, (((1,), (1,)), ((), ())), preferred_element_type=F32
             )
             out = nd[:, :width] / nd[:, width:]
-            heads[h] = out
+            heads[h] = out * gain_ref[pl.ds(h, 1), :]
             return acc + out * out
 
         return lax.fori_loop(0, per, head, acc)
@@ -324,11 +325,11 @@
         send_up(p - 2)
         states(p)
     tot_pair.start()
-    send_up(PHASES - 2)
     tot_pair.wait_recv()
     tot_chip[...] = tot[c] + tot_got[c]
     start(tot_ups)
     tot_up[z] = tot_chip[z]
+    send_up(PHASES - 2)
     send_up(PHASES - 1)
 
     q_load.wait()
@@ -337,16 +338,17 @@
         copy.wait_send()
     send_across(0)
     local_heads(heads_here - 2, heads_here)
-    for p in range(1, PHASES):
-        if p == PHASES - 1:
-            gather_row(tot_ups, tot_up, tot_across.at[XS], tot_across.at[x], tot_xs)
+    for p in range(1, PHASES - 1):
         send_across(p)
         sent(ups[p - 1])
-        if p == PHASES - 1:
-            give_back(tot_xs, tot_across, tot_up, tot_down, tot_back.at[z], tot_downs)
+        if p == 1:
+            gather_row(tot_ups, tot_up, tot_across.at[XS], tot_across.at[x], tot_xs)
         send_down(p - 1)
         sent(xs[p - 1])
-    for copies in (ups[PHASES - 1], tot_ups, tot_xs):
+    give_back(tot_xs, tot_across, tot_up, tot_down, tot_back.at[z], tot_downs)
+    send_down(PHASES - 2)
+    send_across(PHASES - 1)
+    for copies in (ups[PHASES - 2], xs[PHASES - 2], ups[PHASES - 1], tot_ups, tot_xs):
         sent(copies)
     send_down(PHASES - 1)
     sent(xs[PHASES - 1])
@@ -390,14 +392,17 @@
     norm_whole.wait_send()
 
 
-def normalize(heads, factor, gain, out_hbm, out, sems):
-    heads_here, _, width = heads.shape
+def normalize(heads, factor, out_hbm, out, sems):
+    heads_here, tok, width = heads.shape
+    parts = sems.shape[0]
+    size = tok // parts
     copies = []
-    scale = factor[...]
-    for h in range(heads_here):
-        cols = slice(h * width, (h + 1) * width)
-        out[:, cols] = (heads[h] * scale * gain[h : h + 1, :]).astype(BF16)
-        copies.append(pltpu.make_async_copy(out.at[:, cols], out_hbm.at[:, cols], sems.at[h]))
+    for i in range(parts):
+        rows = pl.ds(i * size, size)
+        scale = factor[rows, :]
+        for h in range(heads_here):
+            out[rows, h * width : (h + 1) * width] = (heads[h, rows, :] * scale).astype(BF16)
+        copies.append(pltpu.make_async_copy(out.at[rows], out_hbm.at[rows], sems.at[i]))
         copies[-1].start()
     for copy in copies:
         copy.wait()
@@ -417,7 +422,7 @@
     heads, factor = pl.pallas_call(
         kernel,
         out_shape=(vm((heads_here, tok, width), F32), vm((tok, width), F32)),
-        in_specs=[hbm, hbm, hbm, onchip],
+        in_specs=[hbm, hbm, hbm, onchip, onchip],
         out_specs=(onchip, onchip),
         scratch_shapes=[
             vm((tok, columns), BF16),
@@ -473,18 +478,17 @@
         ],
         compiler_params=pltpu.CompilerParams(collective_id=0, has_side_effects=True),
         name="prefix_attention",
-    )(queries, keys, values, seeds)
+    )(queries, keys, values, seeds, gain.reshape(heads_here, width))
     return pl.pallas_call(
         normalize,
         out_shape=jax.ShapeDtypeStruct((tok, columns), BF16),
-        in_specs=[onchip, onchip, onchip],
+        in_specs=[onchip, onchip],
         out_specs=hbm,
-        scratch_shapes=[vm((tok, columns), BF16), dma((heads_here,))],
+        scratch_shapes=[vm((tok, columns), BF16), dma((4,))],
         name="normalize",
     )(
         pltpu.with_memory_space_constraint(heads, pltpu.VMEM),
         pltpu.with_memory_space_constraint(factor, pltpu.VMEM),
-        gain.reshape(heads_here, width),
     )
 
 

time: 44 us -> 43.1 us (0.980)
  Pallas kernels: 43.8 us -> 42.9 us
    pallas_call x1, Pallas kernels: 1.57 us -> 0.85 us  [per_device(): pl.pallas_call(normalize, out_shape=jax.ShapeDtypeStruct((tok, columns),...]
where the time goes in v3:
time: 43.1 us; the launch traced here: 42.9 us
  Pallas kernels  42.9 us (100%)
    pallas_call x1, Pallas kernels, per_device(): pl.pallas_call(kernel, out_shape=(vm((heads_here, tok, width), F32), vm((...  42 us

profile of v3, /device:TPU:1, one launch (start us, length us, event | category | flops | bytes accessed | tf_op | source)
XLA Modules:
  0.0 42.9 jit_solution(3214400792290000735)
XLA Ops:
  0.0 42.0 %prefix_attention.1 = (f32[8,256,128]{2,1,0:T(8,128)S(1)}, f32[256,128]{1,0:T(8,128)S(1)}) custom-call(bf16[256,1024]{1,0:T(8,128)(2,1)} %q_hbm.1, bf16[256,1024]{1,0:T(8,128)(2,1)} %k_hbm.1, bf16[256,1024]{1,0:T(8,128)(2,1)} %v_hbm.1, bf16[8,256]{1,0:T(8,128)(2,1)} %seeds_ref.1, f32[8,128]{1,0:T(8,128)} %bitcast.1), custom_call_target="tpu_custom_call" | custom-call | tf_op jit(solution)/shard_map/prefix_attention/pallas_call | solution.py:422
  42.1 0.8 %normalize.1 = bf16[256,1024]{1,0:T(8,128)(2,1)} custom-call(f32[8,256,128]{2,1,0:T(8,128)S(1)} %get-tuple-element.7.heads, f32[256,128]{1,0:T(8,128)S(1)} %get-tuple-element.8.factor), custom_call_target="tpu_custom_call" | custom-call | tf_op jit(solution)/shard_map/normalize/pallas_call | solution.py:482
